TPU v7x, 32 devices: a whole 2x2x4 slice. The times are simulated.
32 devices in a mesh: dp: 4 (over z), mp: 8 (over y, x, core).
Axes of the slice: x: 2, y: 2, z: 4, core: 2. Of those that a mesh axis runs over, the one named last changes fastest.
Arguments:
- behaviors: bfloat16 [32, 2048, 1024], P('dp', 'mp'), may hold values from -8 to 8
- candidates: bfloat16 [32, 2048, 128], P('dp', 'mp'), may hold values from -12 to 12
- lengths: int32 [32], P('dp'), may hold values from 128 to 1024
- bilinear: bfloat16 [2048, 2048], P('mp'), may hold values from -1 to 2
- norm_gain: float32 [2048], replicated, may hold values from 0.1 to 1.9
- w_gate: bfloat16 [2048, 8192], P('dp', 'mp'), may hold values from -0.125 to 0.125
- w_up: bfloat16 [2048, 8192], P('dp', 'mp'), may hold values from -0.125 to 0.125
- w_down: bfloat16 [8192, 2048], P('mp', 'dp'), may hold values from -0.0625 to 0.0625
Outputs:
- interest: bfloat16 [32, 2048, 128], P('dp', 'mp')
All inputs are finite; a program needn't handle non-finite values.
Results may differ from a plain program's by a relative error of at most 0.015.
Values may be sent and summed in bfloat16 or wider, within the bound.
No kernel may reach another device: no remote copies, remote signals or barrier semaphores. Data moves between devices by JAX's collectives and lax.ppermute only.
A program may use at most 64 MiB of HBM per device.

v0:
```python
import math
import jax
import jax.numpy as jnp
from jax import lax
from jax.sharding import PartitionSpec as P


def attention_weights(scores, live):
    masked = jnp.where(live, scores, -1e30)
    highest = jnp.max(masked, axis=-1, keepdims=True)
    expons = jnp.where(live, jnp.exp(masked - highest), 0.0)
    return (expons / jnp.sum(expons, axis=-1, keepdims=True)).astype(jnp.bfloat16)


def shards(behaviors, candidates, lengths, bilinear, norm_gain, w_gate, w_up, w_down):
    user_count, width_part, cand_count = candidates.shape
    feature_width = bilinear.shape[1]
    behavior_count = behaviors.shape[2]
    query_part = jnp.einsum(
        "ek,ukc->uec",
        bilinear,
        lax.all_gather(candidates, "mp", axis=1, tiled=True),
        preferred_element_type=jnp.float32,
    )
    query = query_part.astype(jnp.bfloat16)
    partial_value = jnp.einsum("ukc,ukl->ucl", query, behaviors, preferred_element_type=jnp.float32)
    scale = 1.0 / math.sqrt(feature_width)
    live = (
        lax.broadcasted_iota(jnp.int32, (user_count, 1, behavior_count), 2) < lengths[:, None, None]
    )
    share = lax.psum_scatter(partial_value, "mp", scatter_dimension=1, tiled=True)
    probs_share = attention_weights(share * scale, live)
    probs = lax.all_gather(probs_share, "mp", axis=1, tiled=True)
    pooled = jnp.einsum(
        "ucl,ukl->ukc", probs, behaviors, preferred_element_type=jnp.float32
    ).astype(jnp.bfloat16)
    whole = lax.all_gather(pooled, "mp", axis=1, tiled=True)
    values = whole.astype(jnp.float32)
    square_mean = jnp.mean(values * values, axis=1, keepdims=True)
    normed = (values * lax.rsqrt(square_mean + 1e-06) * norm_gain[None, :, None]).astype(
        jnp.bfloat16
    )
    gate = jnp.einsum(
        "ukc,kf->ucf",
        normed,
        lax.all_gather(w_gate, "dp", axis=0, tiled=True),
        preferred_element_type=jnp.float32,
    )
    upward = jnp.einsum(
        "ukc,kf->ucf",
        normed,
        lax.all_gather(w_up, "dp", axis=0, tiled=True),
        preferred_element_type=jnp.float32,
    )
    hidden = (jax.nn.silu(gate) * upward).astype(jnp.bfloat16)
    down_full = lax.all_gather(w_down, "dp", axis=1, tiled=True)
    result = lax.psum_scatter(
        jnp.einsum("ucf,fk->kuc", hidden, down_full, preferred_element_type=jnp.float32).astype(
            jnp.bfloat16
        ),
        "mp",
        scatter_dimension=0,
        tiled=True,
    ).astype(jnp.float32)
    return jnp.transpose(result, (1, 0, 2)).astype(jnp.bfloat16)


def solution(mesh):
    return jax.shard_map(
        shards,
        mesh=mesh,
        in_specs=(
            P("dp", "mp", None),
            P("dp", "mp", None),
            P("dp"),
            P("mp", None),
            P(),
            P("dp", "mp"),
            P("dp", "mp"),
            P("mp", "dp"),
        ),
        out_specs=P("dp", "mp", None),
        check_vma=False,
    )
```

profile of v0, /device:TPU:0, one launch (start us, length us, event | category | flops | bytes accessed | tf_op | source)
XLA Modules:
  0.0 498.7 jit_solution(1023455317639719504)
XLA Ops:
  6.5 0.7 all-gather.7.cloned.1.call-update
  7.3 0.0 reduce-scatter.3.cloned.1.call-start
  7.3 41.3 %all-gather.7.cloned.1.call-done = bf16[8,2048,128]{2,1,0:T(8,128)(2,1)} async-done(((bf16[8,256,128]{2,1,0:T(8,128)(2,1)}), bf16[8,2048,128]{2,1,0:T(8,128)(2,1)}) %all-gather.7.cloned.1.call-update) | async-done | bytes 4194320 | tf_op jit(solution)/shard_map/all_gather | solution.py:22
  48.6 8.2 %fusion.24 = f32[8,128,1024]{2,1,0:T(8,128)} fusion(bf16[8,256,1024]{2,1,0:T(8,128)(2,1)} %param.8, bf16[8,2048,128]{2,1,0:T(8,128)(2,1)} %all-gather.7.cloned.1.call-done, bf16[256,2048]{1,0:T(8,128)(2,1)S(1)} %copy-done), kind=kOutput, calls=%fused_computation.18 | convolution fusion | flops 1610874880 | bytes 13631488 | tf_op jit(solution)/shard_map/ukc,ukl->ucl/dot_general | solution.py:26
  56.7 0.0 reduce-scatter.3.cloned.1.call-update
  56.8 0.0 all-gather.9.cloned.1.call-start
  56.8 0.6 copy-done.1
  57.4 0.1 iota_compare_fusion
  57.5 50.5 %reduce-scatter.3.cloned.1.call-done = f32[8,16,1024]{2,1,0:T(8,128)} async-done(((f32[8,128,1024]{2,1,0:T(8,128)}), f32[8,16,1024]{2,1,0:T(8,128)}) %reduce-scatter.3.cloned.1.call-update) | async-done | bytes 524304 | tf_op jit(solution)/shard_map/reduce_scatter | solution.py:31
  108.0 1.7 fusion.37
  109.7 0.8 divide_convert_fusion
  110.5 0.0 all-gather.9.cloned.1.call-update
  110.6 0.0 all-gather.11.cloned.1.call-start
  110.6 27.9 %all-gather.9.cloned.1.call-done = bf16[8,128,1024]{2,1,0:T(8,128)(2,1)} async-done(((bf16[8,16,1024]{2,1,0:T(8,128)(2,1)}), bf16[8,128,1024]{2,1,0:T(8,128)(2,1)}) %all-gather.9.cloned.1.call-update) | async-done | bytes 2097168 | tf_op jit(solution)/shard_map/all_gather | solution.py:33
  138.5 5.2 %fusion.27 = bf16[8,256,128]{1,2,0:T(8,128)(2,1)} fusion(bf16[8,128,1024]{2,1,0:T(8,128)(2,1)} %all-gather.9.cloned.1.call-done, bf16[8,256,1024]{2,1,0:T(8,128)(2,1)} %param.8), kind=kOutput, calls=%fused_computation.21 | convolution fusion | flops 537133056 | bytes 6815744 | tf_op jit(solution)/shard_map/ucl,ukl->ukc/dot_general | solution.py:34
  143.7 0.0 all-gather.13.cloned.1.call-start
  143.7 0.5 all-gather.13.cloned.1.call-update
  144.3 0.0 all-gather.15.cloned.1.call-start
  144.3 0.5 all-gather.15.cloned.1.call-update
  144.8 0.0 all-gather.17.cloned.1.call-start
  144.9 0.7 all-gather.17.cloned.1.call-update
  145.6 0.2 reduce-scatter.5.cloned.1.call-start
  145.8 35.4 %all-gather.11.cloned.1.call-done = bf16[8,2048,128]{1,2,0:T(8,128)(2,1)} async-done(((bf16[8,256,128]{1,2,0:T(8,128)(2,1)}), bf16[8,2048,128]{1,2,0:T(8,128)(2,1)}) %all-gather.11.cloned.1.call-update) | async-done | bytes 4194320 | tf_op jit(solution)/shard_map/all_gather | solution.py:37
  181.2 3.1 fusion.1
  184.3 79.1 %all-gather.13.cloned.1.call-done = bf16[2048,1024]{1,0:T(8,128)(2,1)} async-done(((bf16[512,1024]{1,0:T(8,128)(2,1)}), bf16[2048,1024]{1,0:T(8,128)(2,1)}) %all-gather.13.cloned.1.call-update) | async-done | bytes 4194320 | tf_op jit(solution)/shard_map/all_gather | solution.py:46
  263.4 9.9 %fusion.8 = f32[8,128,1024]{2,1,0:T(8,128)} fusion(bf16[2048,1024]{1,0:T(8,128)(2,1)} %all-gather.13.cloned.1.call-done, bf16[8,2048,128]{1,2,0:T(8,128)(2,1)} %all-gather.11.cloned.1.call-done, f32[2048]{0:T(1024)S(1)} %copy-done.2, f32[8,128]{1,0:T(8,128)S(1)} %add_rsqrt_fusion), kind=kOutput, calls=%fused_computation.10 | convolution fusion | flops 4303355904 | bytes 12595200 | tf_op jit(solution)/shard_map/ukc,kf->ucf/dot_general | solution.py:43
  273.3 70.7 %all-gather.15.cloned.1.call-done = bf16[2048,1024]{1,0:T(8,128)(2,1)} async-done(((bf16[512,1024]{1,0:T(8,128)(2,1)}), bf16[2048,1024]{1,0:T(8,128)(2,1)}) %all-gather.15.cloned.1.call-update) | async-done | bytes 4194320 | tf_op jit(solution)/shard_map/all_gather | solution.py:52
  344.0 80.8 %all-gather.17.cloned.1.call-done = bf16[1024,2048]{1,0:T(8,128)(2,1)} async-done(((bf16[1024,512]{1,0:T(8,128)(2,1)}), bf16[1024,2048]{1,0:T(8,128)(2,1)}) %all-gather.17.cloned.1.call-update) | async-done | bytes 4194320 | tf_op jit(solution)/shard_map/all_gather | solution.py:56
  424.9 15.2 %convert_bitcast_fusion = bf16[2048,8,128]{0,2,1:T(8,128)(2,1)} fusion(bf16[1024,2048]{1,0:T(8,128)(2,1)} %all-gather.17.cloned.1.call-done, f32[8,128,1024]{2,1,0:T(8,128)} %fusion.8, bf16[2048,1024]{1,0:T(8,128)(2,1)} %all-gather.15.cloned.1.call-done, bf16[8,2048,128]{1,2,0:T(8,128)(2,1)} %all-gather.11.cloned.1.call-done, f32[2048]{0:T(1024)S(1)} %copy-done.2, ...), kind=kOutput, calls=%fused_computation.12 | convolution fusion | flops 8606711808 | bytes 20983808 | tf_op jit(solution)/shard_map/ucf,fk->kuc/dot_general | solution.py:58
  440.1 0.0 reduce-scatter.5.cloned.1.call-update
  440.1 49.7 %reduce-scatter.5.cloned.1.call-done = bf16[256,8,128]{0,2,1:T(8,128)(2,1)} async-done(((bf16[2048,8,128]{0,2,1:T(8,128)(2,1)}), bf16[256,8,128]{0,2,1:T(8,128)(2,1)}) %reduce-scatter.5.cloned.1.call-update) | async-done | bytes 524304 | tf_op jit(solution)/shard_map/reduce_scatter | solution.py:57
  489.8 2.0 copy.9
  (8 shorter events, 0.0 us)
Async XLA Ops:
  6.5 42.0 %copy-start = (bf16[256,2048]{1,0:T(8,128)(2,1)S(1)}, bf16[256,2048]{1,0:T(8,128)(2,1)}, u32[]{:S(2)}) copy-start(bf16[256,2048]{1,0:T(8,128)(2,1)} %param.11) | copy-start | bytes 3145732
  6.5 42.0 %all-gather.7.cloned.1.call-start = ((), (), s32[]{:S(2)}) async-start(), calls=%async_computation.2 | async-start | bytes 4718592 | tf_op jit(solution)/shard_map/all_gather | solution.py:22
  7.3 100.8 %reduce-scatter.3.cloned.1.call-start = ((), (), s32[]{:S(2)}) async-start(), calls=%async_computation.3 | async-start | bytes 4718592 | tf_op jit(solution)/shard_map/reduce_scatter | solution.py:31
  56.7 0.7 copy-start.1
  56.8 81.7 %all-gather.9.cloned.1.call-start = ((), (), s32[]{:S(2)}) async-start(), calls=%async_computation.4 | async-start | bytes 2359296 | tf_op jit(solution)/shard_map/all_gather | solution.py:33
  110.6 70.6 %all-gather.11.cloned.1.call-start = ((), (), s32[]{:S(2)}) async-start(), calls=%async_computation.5 | async-start | bytes 4718592 | tf_op jit(solution)/shard_map/all_gather | solution.py:37
  143.7 119.7 %copy-start.2 = (f32[2048]{0:T(1024)S(1)}, f32[2048]{0:T(1024)}, u32[]{:S(2)}) copy-start(f32[2048]{0:T(1024)} %param.12) | copy-start | bytes 24580
  143.7 119.7 %all-gather.13.cloned.1.call-start = ((), (), s32[]{:S(2)}) async-start(), calls=%async_computation.6 | async-start | bytes 5242880 | tf_op jit(solution)/shard_map/all_gather | solution.py:46
  144.3 199.8 %all-gather.15.cloned.1.call-start = ((), (), s32[]{:S(2)}) async-start(), calls=%async_computation.7 | async-start | bytes 5242880 | tf_op jit(solution)/shard_map/all_gather | solution.py:52
  144.8 280.0 %all-gather.17.cloned.1.call-start = ((), (), s32[]{:S(2)}) async-start(), calls=%async_computation.8 | async-start | bytes 5242880 | tf_op jit(solution)/shard_map/all_gather | solution.py:56
  145.6 344.2 %reduce-scatter.5.cloned.1.call-start = ((), (), s32[]{:S(2)}) async-start(), calls=%async_computation.9 | async-start | bytes 4718592 | tf_op jit(solution)/shard_map/reduce_scatter | solution.py:57
Sparse Core Ops, SparseCore 0:
  9.2 39.2 all-gather.6
  56.9 51.0 reduce-scatter.2
  110.7 27.7 all-gather.8
  143.8 37.3 all-gather.10
  182.6 80.7 all-gather.12
  264.8 79.2 all-gather.14
  345.6 79.2 all-gather.16
  440.2 49.5 reduce-scatter.4
where the time goes:
time: 499 us
  waiting for transfers between devices  438 us (88%)
  matrix products  38.4 us (8%)
  between operations  13.5 us (3%)
  other arithmetic  5.68 us (1%)
    all_gather x1, waiting for transfers between devices, shards(): down_full = lax.all_gather(w_down, 'dp', axis=1, tiled=True)  80.8 us
    all_gather x1, waiting for transfers between devices, shards(): lax.all_gather(w_gate, 'dp', axis=0, tiled=True)  79.1 us
    all_gather x1, waiting for transfers between devices, shards(): lax.all_gather(w_up, 'dp', axis=0, tiled=True)  70.7 us
    reduce_scatter x1, waiting for transfers between devices, shards(): lax.psum_scatter(partial_value, 'mp', scatter_dimension=1, tiled=True)  50.5 us
    reduce_scatter x1, waiting for transfers between devices, shards(): lax.psum_scatter(jnp.einsum('ucf,fk->kuc', hidden, down_full, preferred_e...  49.7 us
    all_gather x1, waiting for transfers between devices, shards(): lax.all_gather(candidates, 'mp', axis=1, tiled=True)  41.3 us
    all_gather x1, waiting for transfers between devices, shards(): whole = lax.all_gather(pooled, 'mp', axis=1, tiled=True)  35.4 us
    all_gather x1, waiting for transfers between devices, shards(): probs = lax.all_gather(probs_share, 'mp', axis=1, tiled=True)  27.9 us
  transfers between devices with their start and end apart: 8, of which 8 were waited for; matrix products, arithmetic and copies ran while one was open for 3% of the time, Pallas kernels for 0%

commit v1 on v0

--- a/solution.py
+++ b/solution.py
@@ -34,7 +34,7 @@
     pooled = jnp.einsum(
         "ucl,ukl->ukc", probs, behaviors, preferred_element_type=jnp.float32
     ).astype(jnp.bfloat16)
-    whole = lax.all_gather(pooled, "mp", axis=1, tiled=True)
+    whole = jnp.concatenate(lax.all_gather(pooled, "mp"), axis=1)
     values = whole.astype(jnp.float32)
     square_mean = jnp.mean(values * values, axis=1, keepdims=True)
     normed = (values * lax.rsqrt(square_mean + 1e-06) * norm_gain[None, :, None]).astype(

time: 499 us -> 492 us (0.986)
  waiting for transfers between devices: 438 us -> 400 us
  local copies, waits for them, and re-layouts: 2.63 us -> 22.3 us
  other arithmetic: 5.68 us -> 12.1 us
    convert_element_type x0 -> x3, local copies, waits for them, and re-layouts: none -> 19.6 us  [the longest x2 18.6 us: shards(): values = whole.astype(jnp.float32)]
    all_gather x1, waiting for transfers between devices: 70.7 us -> 54 us  [shards(): lax.all_gather(w_up, 'dp', axis=0, tiled=True)]
    dot_general x0 -> x1, matrix products: none -> 11.1 us  [shards(): jnp.einsum('ukc,kf->ucf', normed, lax.all_gather(w_up, 'dp', axis=0, tile...]
    all_gather x1, waiting for transfers between devices: 80.8 us -> 70 us  [shards(): down_full = lax.all_gather(w_down, 'dp', axis=1, tiled=True)]
    all_gather x1, waiting for transfers between devices: 79.1 us -> 69.6 us  [shards(): lax.all_gather(w_gate, 'dp', axis=0, tiled=True)]
    dot_general x1, matrix products: 15.2 us -> 8.32 us  [shards(): jnp.einsum('ucf,fk->kuc', hidden, down_full, preferred_element_type=jnp.f...]
    convert_element_type x0 -> x1, other arithmetic: none -> 6.49 us  [shards(): values = whole.astype(jnp.float32)]
  transfers between devices with their start and end apart: 8 -> 8, of which waited for: 8 -> 8; matrix products, arithmetic and copies ran while one was open for 3% -> 10% of each run, Pallas kernels for 0% -> 0%
where the time goes in v1:
time: 492 us; the launch traced here: 491 us
  waiting for transfers between devices  400 us (81%)
  matrix products  42.7 us (9%)
  local copies, waits for them, and re-layouts  22.3 us (5%)
  between operations  13.5 us (3%)
  other arithmetic  12.1 us (2%)
    all_gather x1, waiting for transfers between devices, shards(): down_full = lax.all_gather(w_down, 'dp', axis=1, tiled=True)  70 us
    all_gather x1, waiting for transfers between devices, shards(): lax.all_gather(w_gate, 'dp', axis=0, tiled=True)  69.6 us
    all_gather x1, waiting for transfers between devices, shards(): lax.all_gather(w_up, 'dp', axis=0, tiled=True)  54 us
    reduce_scatter x1, waiting for transfers between devices, shards(): lax.psum_scatter(partial_value, 'mp', scatter_dimension=1, tiled=True)  50.5 us
    reduce_scatter x1, waiting for transfers between devices, shards(): lax.psum_scatter(jnp.einsum('ucf,fk->kuc', hidden, down_full, preferred_e...  49.7 us
    all_gather x1, waiting for transfers between devices, shards(): lax.all_gather(candidates, 'mp', axis=1, tiled=True)  41.3 us
    all_gather x1, waiting for transfers between devices, shards(): whole = jnp.concatenate(lax.all_gather(pooled, 'mp'), axis=1)  34.6 us
    all_gather x1, waiting for transfers between devices, shards(): probs = lax.all_gather(probs_share, 'mp', axis=1, tiled=True)  27.9 us
  transfers between devices with their start and end apart: 8, of which 8 were waited for; matrix products, arithmetic and copies ran while one was open for 10% of the time, Pallas kernels for 0%

profile of v1, /device:TPU:0, one launch (start us, length us, event | category | flops | bytes accessed | tf_op | source)
XLA Modules:
  0.0 491.2 jit_solution(14215270502150349144)
XLA Ops:
  6.5 0.7 all-gather.8.cloned.1.call-update
  7.3 0.0 reduce-scatter.3.cloned.1.call-start
  7.3 41.3 %all-gather.8.cloned.1.call-done = bf16[8,2048,128]{2,1,0:T(8,128)(2,1)} async-done(((bf16[8,256,128]{2,1,0:T(8,128)(2,1)}), bf16[8,2048,128]{2,1,0:T(8,128)(2,1)}) %all-gather.8.cloned.1.call-update) | async-done | bytes 4194320 | tf_op jit(solution)/shard_map/all_gather | solution.py:22
  48.6 8.2 %fusion.13 = f32[8,128,1024]{2,1,0:T(8,128)} fusion(bf16[8,256,1024]{2,1,0:T(8,128)(2,1)} %param.8, bf16[8,2048,128]{2,1,0:T(8,128)(2,1)} %all-gather.8.cloned.1.call-done, bf16[256,2048]{1,0:T(8,128)(2,1)S(1)} %copy-done), kind=kOutput, calls=%fused_computation.16 | convolution fusion | flops 1610874880 | bytes 13631488 | tf_op jit(solution)/shard_map/ukc,ukl->ucl/dot_general | solution.py:26
  56.8 0.0 all-gather.10.cloned.1.call-start
  56.8 0.6 copy-done.2
  57.4 0.1 iota_compare_fusion
  57.5 50.5 %reduce-scatter.3.cloned.1.call-done = f32[8,16,1024]{2,1,0:T(8,128)} async-done(((f32[8,128,1024]{2,1,0:T(8,128)}), f32[8,16,1024]{2,1,0:T(8,128)}) %reduce-scatter.3.cloned.1.call-update) | async-done | bytes 524304 | tf_op jit(solution)/shard_map/reduce_scatter | solution.py:31
  108.0 1.6 fusion.25
  109.7 0.8 divide_convert_fusion
  110.5 0.0 all-gather.18.cloned.1.call-start
  110.6 27.9 %all-gather.10.cloned.1.call-done = bf16[8,128,1024]{2,1,0:T(8,128)(2,1)} async-done(((bf16[8,16,1024]{2,1,0:T(8,128)(2,1)}), bf16[8,128,1024]{2,1,0:T(8,128)(2,1)}) %all-gather.10.cloned.1.call-update) | async-done | bytes 2097168 | tf_op jit(solution)/shard_map/all_gather | solution.py:33
  138.4 4.4 fusion.16
  142.8 1.0 copy.11
  143.8 0.0 all-gather.14.cloned.1.call-start
  143.9 0.5 all-gather.14.cloned.1.call-update
  144.5 0.5 all-gather.12.cloned.1.call-update
  145.0 0.7 all-gather.16.cloned.1.call-update
  145.7 0.2 reduce-scatter.5.cloned.1.call-start
  146.0 34.6 %all-gather.18.cloned.1.call-done = bf16[64,256,128]{2,1,0:T(8,128)(2,1)} async-done(((bf16[8,256,128]{2,1,0:T(8,128)(2,1)}), bf16[64,256,128]{2,1,0:T(8,128)(2,1)}) %all-gather.18.cloned.1.call-update) | async-done | bytes 4194320 | tf_op jit(solution)/shard_map/all_gather | solution.py:37
  180.6 6.5 %convert_bitcast_fusion = f32[8,8,256,128]{3,2,0,1:T(8,128)} fusion(bf16[64,256,128]{2,1,0:T(8,128)(2,1)} %all-gather.18.cloned.1.call-done), kind=kLoop, calls=%fused_computation.2 | loop fusion | flops 2097152 | bytes 12582912 | tf_op jit(solution)/shard_map/convert_element_type | solution.py:38
  187.1 9.3 %copy.12 = f32[8,8,256,128]{2,1,3,0:T(8,128)} copy(f32[8,8,256,128]{3,2,0,1:T(8,128)} %convert_bitcast_fusion) | data formatting | bytes 16777216 | tf_op jit(solution)/shard_map/convert_element_type | solution.py:38
  196.4 9.3 %reshape.33 = f32[8,2048,128]{1,2,0:T(8,128)} reshape(f32[8,8,256,128]{2,1,3,0:T(8,128)} %copy.12) | data formatting | bytes 16777216 | tf_op jit(solution)/shard_map/convert_element_type | solution.py:38
  205.7 3.0 fusion.1
  208.7 54.0 %all-gather.14.cloned.1.call-done = bf16[2048,1024]{1,0:T(8,128)(2,1)} async-done(((bf16[512,1024]{1,0:T(8,128)(2,1)}), bf16[2048,1024]{1,0:T(8,128)(2,1)}) %all-gather.14.cloned.1.call-update) | async-done | bytes 4194320 | tf_op jit(solution)/shard_map/all_gather | solution.py:52
  262.8 11.1 %fusion.4 = f32[8,128,1024]{2,1,0:T(8,128)} fusion(bf16[2048,1024]{1,0:T(8,128)(2,1)} %all-gather.14.cloned.1.call-done, f32[8,2048,128]{1,2,0:T(8,128)} %reshape.33, f32[2048]{0:T(1024)S(1)} %copy-done.3, f32[8,128]{1,0:T(8,128)S(1)} %add_rsqrt_fusion), kind=kOutput, calls=%fused_computation.7 | convolution fusion | flops 4301258752 | bytes 16789504 | tf_op jit(solution)/shard_map/ukc,kf->ucf/dot_general | solution.py:49
  273.8 69.6 %all-gather.12.cloned.1.call-done = bf16[2048,1024]{1,0:T(8,128)(2,1)} async-done(((bf16[512,1024]{1,0:T(8,128)(2,1)}), bf16[2048,1024]{1,0:T(8,128)(2,1)}) %all-gather.12.cloned.1.call-update) | async-done | bytes 4194320 | tf_op jit(solution)/shard_map/all_gather | solution.py:46
  343.4 10.8 %multiply_convert_fusion.1 = bf16[8,128,1024]{2,1,0:T(8,128)(2,1)S(1)} fusion(f32[8,128,1024]{2,1,0:T(8,128)} %fusion.4, bf16[2048,1024]{1,0:T(8,128)(2,1)} %all-gather.12.cloned.1.call-done, f32[8,2048,128]{1,2,0:T(8,128)} %reshape.33, f32[2048]{0:T(1024)S(1)} %copy-done.3, f32[8,128]{1,0:T(8,128)S(1)} %add_rsqrt_fusion), kind=kOutput, calls=%fused_computation.12 | convolution fusion | flops 4307550208 | bytes 18886656 | tf_op jit(solution)/shard_map/ukc,kf->ucf/dot_general | solution.py:43
  354.3 70.0 %all-gather.16.cloned.1.call-done = bf16[1024,2048]{1,0:T(8,128)(2,1)} async-done(((bf16[1024,512]{1,0:T(8,128)(2,1)}), bf16[1024,2048]{1,0:T(8,128)(2,1)}) %all-gather.16.cloned.1.call-update) | async-done | bytes 4194320 | tf_op jit(solution)/shard_map/all_gather | solution.py:56
  424.3 8.3 %convert_bitcast_fusion.1 = bf16[2048,8,128]{0,2,1:T(8,128)(2,1)} fusion(bf16[8,128,1024]{2,1,0:T(8,128)(2,1)S(1)} %multiply_convert_fusion.1, bf16[1024,2048]{1,0:T(8,128)(2,1)} %all-gather.16.cloned.1.call-done), kind=kOutput, calls=%fused_computation.11 | convolution fusion | flops 4297064448 | bytes 10485760 | tf_op jit(solution)/shard_map/ucf,fk->kuc/dot_general | solution.py:58
  432.6 49.7 %reduce-scatter.5.cloned.1.call-done = bf16[256,8,128]{0,2,1:T(8,128)(2,1)} async-done(((bf16[2048,8,128]{0,2,1:T(8,128)(2,1)}), bf16[256,8,128]{0,2,1:T(8,128)(2,1)}) %reduce-scatter.5.cloned.1.call-update) | async-done | bytes 524304 | tf_op jit(solution)/shard_map/reduce_scatter | solution.py:57
  482.3 2.0 copy.13
  (15 shorter events, 0.2 us)
Async XLA Ops:
  6.5 42.0 %copy-start = (bf16[256,2048]{1,0:T(8,128)(2,1)S(1)}, bf16[256,2048]{1,0:T(8,128)(2,1)}, u32[]{:S(2)}) copy-start(bf16[256,2048]{1,0:T(8,128)(2,1)} %param.11) | copy-start | bytes 3145732
  6.5 42.0 %all-gather.8.cloned.1.call-start = ((), (), s32[]{:S(2)}) async-start(), calls=%async_computation.2 | async-start | bytes 4718592 | tf_op jit(solution)/shard_map/all_gather | solution.py:22
  7.3 100.8 %reduce-scatter.3.cloned.1.call-start = ((), (), s32[]{:S(2)}) async-start(), calls=%async_computation.3 | async-start | bytes 4718592 | tf_op jit(solution)/shard_map/reduce_scatter | solution.py:31
  56.7 0.7 copy-start.2
  56.8 81.7 %all-gather.10.cloned.1.call-start = ((), (), s32[]{:S(2)}) async-start(), calls=%async_computation.4 | async-start | bytes 2359296 | tf_op jit(solution)/shard_map/all_gather | solution.py:33
  110.5 70.0 %all-gather.18.cloned.1.call-start = ((), (), s32[]{:S(2)}) async-start(), calls=%async_computation.9 | async-start | bytes 4718592 | tf_op jit(solution)/shard_map/all_gather | solution.py:37
  143.8 118.9 %all-gather.14.cloned.1.call-start = ((), (), s32[]{:S(2)}) async-start(), calls=%async_computation.6 | async-start | bytes 5242880 | tf_op jit(solution)/shard_map/all_gather | solution.py:52
  144.4 199.0 %all-gather.12.cloned.1.call-start = ((), (), s32[]{:S(2)}) async-start(), calls=%async_computation.5 | async-start | bytes 5242880 | tf_op jit(solution)/shard_map/all_gather | solution.py:46
  145.0 279.3 %all-gather.16.cloned.1.call-start = ((), (), s32[]{:S(2)}) async-start(), calls=%async_computation.7 | async-start | bytes 5242880 | tf_op jit(solution)/shard_map/all_gather | solution.py:56
  145.7 336.6 %reduce-scatter.5.cloned.1.call-start = ((), (), s32[]{:S(2)}) async-start(), calls=%async_computation.8 | async-start | bytes 4718592 | tf_op jit(solution)/shard_map/reduce_scatter | solution.py:57
  205.7 57.1 %copy-start.3 = (f32[2048]{0:T(1024)S(1)}, f32[2048]{0:T(1024)}, u32[]{:S(2)}) copy-start(f32[2048]{0:T(1024)} %param.12) | copy-start | bytes 24580
  424.3 60.1 %copy-start.1 = (bf16[256,2048]{1,0:T(8,128)(2,1)S(1)}, bf16[256,2048]{1,0:T(8,128)(2,1)}, u32[]{:S(2)}) copy-start(bf16[256,2048]{1,0:T(8,128)(2,1)} %param.11) | copy-start | bytes 3145732
Sparse Core Ops, SparseCore 0:
  9.2 39.2 all-gather.7
  56.9 51.0 reduce-scatter.2
  110.6 27.7 all-gather.9
  144.0 36.5 all-gather.17
  182.0 80.7 all-gather.13
  264.2 79.2 all-gather.11
  345.0 79.2 all-gather.15
  432.7 49.5 reduce-scatter.4
